TPU v7x, 128 devices: a whole 4x4x4 slice. The times are simulated.
128 devices in a mesh: pool: 32 (over x, z, core), exp: 4 (over y).
Axes of the slice: x: 4, y: 4, z: 4, core: 2. Of those that a mesh axis runs over, the one named last changes fastest.
Arguments:
- tokens: bfloat16 [512, 1024], P('pool'), as said below
- block_table: int32 [512, 128], replicated, may hold values from -1 to 4607, as said below
- lengths: int32 [512], replicated, may hold values from 1 to 16384, as said below
- k_cache: bfloat16 [4096, 128, 512], P('pool', None, 'exp'), as said below
- v_cache: bfloat16 [4096, 128, 512], P('pool', None, 'exp'), may hold values from -9 to 9
- hidden_store: bfloat16 [512, 128, 1024], P('pool'), may hold values from -6 to 6
- norm_attn: bfloat16 [1024], replicated, may hold values from 0.5 to 1.5
- w_query: bfloat16 [1024, 1024], P(None, 'exp'), as said below
- w_key: bfloat16 [1024, 512], P(None, 'exp'), may hold values from -0.1875 to 0.1875
- w_value: bfloat16 [1024, 512], P(None, 'exp'), may hold values from -0.1875 to 0.1875
- w_out: bfloat16 [1024, 1024], P('exp'), may hold values from -0.1875 to 0.1875
- norm_moe: bfloat16 [1024], replicated, may hold values from 0.5 to 1.5
- expert_ids: int32 [512, 8], P('pool'), may hold values from 0 to 31, all different within a row; in each aligned block of 16 rows (0 to 15, 16 to 31, ...) at most 8 rows name the same one
- gate_weights: float32 [512, 8], P('pool'), may hold values from 0.1 to 1
- w_gate: bfloat16 [32, 1024, 512], P('pool'), may hold values from -0.1875 to 0.1875
- w_up: bfloat16 [32, 1024, 512], P('pool'), may hold values from -0.1875 to 0.1875
- w_down: bfloat16 [32, 512, 1024], P('pool'), may hold values from -0.25 to 0.25
Outputs:
- layer_out: bfloat16 [512, 1024], P('pool', 'exp')
Inputs may be any that keep to these rules, and one draw needn't show every extreme that they name: `block_table`: every block number 0 to 4607 stands exactly once in the table; a request's blocks fill the start of its row and -1 fills the rest; each request has 1 to 128 blocks and some request has exactly 128. `lengths`: A request with n blocks has a length above (n - 1) * 128 and at most n * 128; some request has the length 16384. `expert_ids`: in the rows of one pool index no expert is named by more than 8 rows. `tokens`: entries lie within -8 to 8. `k_cache`: entries lie within -8 to 8. `w_query`: entries are of magnitude below 7 / sqrt(1024).
All inputs are finite; a program needn't handle non-finite values.
Results may differ from a plain program's by a relative error of at most 0.009.
Values may be sent and summed in bfloat16 or wider, within the bound.
No kernel may reach another device: no remote copies, remote signals or barrier semaphores. Data moves between devices by JAX's collectives and lax.ppermute only.
A program may use at most 128 MiB of HBM per device.

v0:
```python
import jax
import jax.numpy as jnp
from jax import lax
from jax.sharding import PartitionSpec as P

HEAD_SIZE = 64
NEG_FILL = -1e30
EPSILON = 1e-05
SCORE_SCALE = 0.125
HIGHEST = lax.Precision.HIGHEST


def merged(value, axis, join):
    pieces = jax.tree.map(lambda part: lax.all_gather(part, axis), value)
    head = jax.tree.map(lambda part: part[0], pieces)
    tail = jax.tree.map(lambda part: part[1:], pieces)
    so_far, _ = lax.scan(lambda so_far, piece: (join(so_far, piece), None), head, tail)
    return so_far


def rms_scale(row_vals, gain_row):
    mean_sq = jnp.mean(row_vals * row_vals, axis=-1, keepdims=True)
    return row_vals * lax.rsqrt(mean_sq + EPSILON) * gain_row


def merge_pair(first, second):
    top_a, sum_a, out_a = first
    top_b, sum_b, out_b = second
    row_top = jnp.maximum(top_a, top_b)
    weight_a = jnp.exp(top_a - row_top)
    weight_b = jnp.exp(top_b - row_top)
    spread = out_a.shape[-1] // top_a.shape[-1]
    merged_out = out_a * jnp.repeat(weight_a, spread, axis=-1) + out_b * jnp.repeat(
        weight_b, spread, axis=-1
    )
    return (row_top, sum_a * weight_a + sum_b * weight_b, merged_out)


def on_device(
    tokens,
    block_table,
    lengths,
    k_cache,
    v_cache,
    hidden_store,
    norm_attn,
    w_query,
    w_key,
    w_value,
    w_out,
    norm_moe,
    expert_ids,
    gate_weights,
    w_gate,
    w_up,
    w_down,
):
    pool_count = lax.axis_size("pool")
    exp_count = lax.axis_size("exp")
    pool_index = lax.axis_index("pool")
    exp_index = lax.axis_index("exp")
    req_dev = tokens.shape[0]
    model_width = tokens.shape[1]
    quarter = model_width // exp_count
    x_rows = tokens.astype(jnp.float32)
    normed = rms_scale(x_rows, norm_attn.astype(jnp.float32)).astype(jnp.bfloat16)
    queries = jnp.dot(normed, w_query, preferred_element_type=jnp.float32).astype(jnp.bfloat16)
    all_queries = lax.all_gather(queries, "pool", axis=0, tiled=True)
    stored_rows = hidden_store.reshape(-1, model_width)
    stored_shape = (hidden_store.shape[0], hidden_store.shape[1], w_key.shape[1])
    key_new = (
        jnp.dot(stored_rows, w_key, preferred_element_type=jnp.float32)
        .astype(jnp.bfloat16)
        .reshape(stored_shape)
    )
    value_new = (
        jnp.dot(stored_rows, w_value, preferred_element_type=jnp.float32)
        .astype(jnp.bfloat16)
        .reshape(stored_shape)
    )
    keys_here = jnp.concatenate([k_cache, key_new], axis=0)
    values_here = jnp.concatenate([v_cache, value_new], axis=0)
    slot_count, page_len, key_width = keys_here.shape
    query_width = queries.shape[1]
    kv_groups = key_width // HEAD_SIZE
    per_group = query_width // key_width
    head_count = query_width // HEAD_SIZE
    requests = block_table.shape[0]
    list_len = block_table.shape[1]
    flat_ids = block_table.reshape(-1)
    entry_index = jnp.arange(requests * list_len, dtype=jnp.int32)
    global_slot = pool_index * slot_count + jnp.arange(slot_count, dtype=jnp.int32)
    found_entry = jnp.sum(
        jnp.where(flat_ids[None, :] == global_slot[:, None], entry_index[None, :], 0), axis=1
    )
    slot_req = found_entry // list_len
    slot_block = found_entry % list_len
    member = slot_req[:, None] == jnp.arange(requests, dtype=jnp.int32)[None, :]
    member_low = member.astype(jnp.bfloat16)
    slot_queries = jnp.dot(member_low, all_queries, preferred_element_type=jnp.float32).astype(
        jnp.bfloat16
    )
    slot_length = jnp.sum(jnp.where(member, lengths[None, :], 0), axis=1)
    q_grouped = slot_queries.reshape(slot_count, kv_groups, per_group, HEAD_SIZE)
    k_grouped = keys_here.reshape(slot_count, page_len, kv_groups, HEAD_SIZE)
    v_grouped = values_here.reshape(slot_count, page_len, kv_groups, HEAD_SIZE)
    scores = (
        jnp.einsum("sgqd,stgd->sgqt", q_grouped, k_grouped, preferred_element_type=jnp.float32)
        * SCORE_SCALE
    )
    positions = slot_block[:, None] * page_len + jnp.arange(page_len, dtype=jnp.int32)[None, :]
    is_valid = (positions < slot_length[:, None])[:, None, None, :]
    masked = jnp.where(is_valid, scores, NEG_FILL)
    block_top = jnp.max(masked, axis=-1)
    weights = jnp.where(is_valid, jnp.exp(masked - block_top[..., None]), 0.0)
    block_sum = jnp.sum(weights, axis=-1)
    block_out = jnp.einsum(
        "sgqt,stgd->sgqd",
        weights.astype(jnp.bfloat16),
        v_grouped,
        preferred_element_type=jnp.float32,
    )
    slot_top = block_top.reshape(slot_count, head_count)
    slot_sum = block_sum.reshape(slot_count, head_count)
    slot_out = block_out.reshape(slot_count, query_width)
    local_top = jnp.max(jnp.where(member[:, :, None], slot_top[:, None, :], NEG_FILL), axis=0)
    own_top = jnp.max(jnp.where(member[:, :, None], local_top[None, :, :], NEG_FILL), axis=1)
    factor = jnp.exp(slot_top - own_top)
    one_hot = member.astype(jnp.float32)
    local_sum = jnp.einsum("sr,sh->rh", one_hot, slot_sum * factor, precision=HIGHEST)
    local_out = jnp.einsum(
        "sr,sc->rc", one_hot, slot_out * jnp.repeat(factor, HEAD_SIZE, axis=1), precision=HIGHEST
    )
    all_top, all_sum, all_out = merged((local_top, local_sum, local_out), "pool", merge_pair)
    row_start = pool_index * req_dev
    total_sum = lax.dynamic_slice_in_dim(all_sum, row_start, req_dev, 0)
    accum = lax.dynamic_slice_in_dim(all_out, row_start, req_dev, 0)
    attended = (accum / jnp.repeat(total_sum, HEAD_SIZE, axis=-1)).astype(jnp.bfloat16)
    projected = lax.psum(jnp.dot(attended, w_out, preferred_element_type=jnp.float32), "exp")
    mixed = x_rows + projected
    normed_moe = rms_scale(mixed, norm_moe.astype(jnp.float32)).astype(jnp.bfloat16)
    top_count = expert_ids.shape[1]
    capacity = min(req_dev, 2 * ((req_dev * top_count + pool_count - 1) // pool_count))
    route_flat = expert_ids.reshape(-1)
    expert_hit = (route_flat[:, None] == jnp.arange(pool_count, dtype=jnp.int32)[None, :]).astype(
        jnp.int32
    )
    slot_rank = jnp.sum(jnp.cumsum(expert_hit, axis=0) * expert_hit, axis=1) - 1
    slot_pos = route_flat * capacity + slot_rank
    placed = (
        slot_pos[:, None] == jnp.arange(pool_count * capacity, dtype=jnp.int32)[None, :]
    ).astype(jnp.float32)
    placed = placed.reshape(req_dev, top_count, pool_count * capacity)
    send_map = jnp.sum(placed, axis=1).astype(jnp.bfloat16)
    combine_map = jnp.einsum("tk,tkc->tc", gate_weights, placed, precision=HIGHEST)
    outgoing = jnp.einsum("tc,td->cd", send_map, normed_moe, preferred_element_type=jnp.float32)
    outgoing = outgoing.astype(jnp.bfloat16).reshape(pool_count, capacity, model_width)
    arrived = lax.all_to_all(outgoing, "pool", split_axis=0, concat_axis=0, tiled=True)
    sources = arrived.shape[0]
    slots_here = arrived.shape[1]
    row_block = arrived.reshape(-1, model_width)
    gate_act = jnp.dot(row_block, w_gate[0], preferred_element_type=jnp.float32)
    up_act = jnp.dot(row_block, w_up[0], preferred_element_type=jnp.float32)
    hidden = (jax.nn.silu(gate_act) * up_act).astype(jnp.bfloat16)
    expert_low = jnp.dot(hidden, w_down[0], preferred_element_type=jnp.float32).astype(jnp.bfloat16)
    expert_low = expert_low.reshape(sources, slots_here, model_width)
    expert_out = lax.dynamic_slice_in_dim(expert_low, exp_index * quarter, quarter, 2)
    returned = lax.all_to_all(expert_out, "pool", split_axis=0, concat_axis=0, tiled=True)
    moe_share = jnp.dot(
        combine_map,
        returned.reshape(pool_count * capacity, quarter).astype(jnp.float32),
        precision=HIGHEST,
    )
    mixed_share = lax.dynamic_slice_in_dim(mixed, exp_index * quarter, quarter, 1)
    return (mixed_share + moe_share).astype(jnp.bfloat16)


def solution(mesh):
    placed = (
        P("pool", None),
        P(),
        P(),
        P("pool", None, "exp"),
        P("pool", None, "exp"),
        P("pool", None, None),
        P(),
        P(None, "exp"),
        P(None, "exp"),
        P(None, "exp"),
        P("exp", None),
        P(),
        P("pool", None),
        P("pool", None),
        P("pool", None, None),
        P("pool", None, None),
        P("pool", None, None),
    )
    return jax.shard_map(
        on_device, mesh=mesh, in_specs=placed, out_specs=P("pool", "exp"), check_vma=False
    )
```

profile of v0, /device:TPU:1, one launch (start us, length us, event | category | flops | bytes accessed | tf_op | source)
XLA Modules:
  0.0 319.9 jit_solution(11277620771074689597)
XLA Ops:
  6.5 6.6 %select_reduce_fusion = s32[144]{0:T(256)S(1)} fusion(s32[65536]{0:T(1024)} %bitcast.87, s32[144]{0:T(256)S(1)} %iota_add_fusion), kind=kLoop, calls=%fused_computation.10 | loop fusion | flops 28311408 | bytes 263296 | tf_op jit(solution)/shard_map/reduce_sum | solution.py:93
  13.3 0.9 select_reduce_fusion.3
  14.9 0.9 fusion.46
  15.8 1.3 convolution_convert_fusion.5
  17.1 27.6 %all_gather.21 = bf16[512,256]{1,0:T(8,128)(2,1)S(1)} all-gather(bf16[16,256]{1,0:T(8,128)(2,1)S(1)} %convolution_convert_fusion.5), channel_id=1, replica_groups=mesh['pool'=32,'exp'=4] {'pool'}, dimensions={0}, use_global_device_ids=true | all-gather | bytes 270336 | tf_op jit(solution)/shard_map/all_gather | solution.py:68
  45.1 3.5 %convolution_convert_fusion.1 = bf16[2048,128]{1,0:T(8,128)(2,1)S(1)} fusion(bf16[2048,1024]{1,0:T(8,128)(2,1)} %bitcast.89, bf16[1024,128]{1,0:T(8,128)(2,1)} %param.27), kind=kOutput, calls=%fused_computation.20 | convolution fusion | flops 537133056 | bytes 4980736 | tf_op jit(solution)/shard_map/dot_general | solution.py:72
  49.6 6.4 %copy.75 = bf16[128,128,128]{1,2,0:T(8,128)(2,1)} copy(bf16[128,128,128]{2,1,0:T(8,128)(2,1)} %param.22) | data formatting | bytes 8388608 | tf_op args[3]
  56.1 3.7 %fusion.67 = (f32[144,2,2]{2,1,0:T(2,128)S(1)}, f32[144,2,2,128]{3,2,1,0:T(2,128)S(1)}) fusion(bf16[144,2,2,64]{3,2,1,0:T(2,128)(2,1)S(1)} %reshape.185, bf16[16,128,2,64]{1,3,2,0:T(8,128)(2,1)S(1)} %copy.77, bf16[128,128,2,64]{1,3,2,0:T(8,128)(2,1)} %bitcast.84, pred[144,128]{1,0:T(8,128)(4,1)S(1)} %add_compare_fusion), kind=kOutput, calls=%fused_computation.105 | convolution fusion | flops 12017088 | bytes 5107968 | tf_op jit(solution)/shard_map/sgqd,stgd->sgqt/dot_general | solution.py:108
  61.0 3.4 %convolution_convert_fusion = bf16[2048,128]{1,0:T(8,128)(2,1)S(1)} fusion(bf16[2048,1024]{1,0:T(8,128)(2,1)} %bitcast.90, bf16[1024,128]{1,0:T(8,128)(2,1)S(1)} %copy-done.6), kind=kOutput, calls=%fused_computation.19 | convolution fusion | flops 537133056 | bytes 4980736 | tf_op jit(solution)/shard_map/dot_general | solution.py:77
  65.5 6.4 %copy.80 = bf16[128,128,128]{1,2,0:T(8,128)(2,1)} copy(bf16[128,128,128]{2,1,0:T(8,128)(2,1)} %param.23) | data formatting | bytes 8388608 | tf_op args[4]
  71.9 4.8 %fusion.7 = f32[144,2,2,64]{3,2,1,0:T(2,128)S(1)} fusion(bf16[16,128,2,64]{1,3,2,0:T(8,128)(2,1)S(1)} %copy.82, bf16[128,128,2,64]{1,3,2,0:T(8,128)(2,1)} %bitcast.85, f32[144,2,2,128]{3,2,1,0:T(2,128)S(1)} %get-tuple-element.103, pred[144,128]{1,0:T(8,128)(4,1)S(1)} %add_compare_fusion, f32[144,2,2]{2,1,0:T(2,128)S(1)} %get-tuple-element.102), kind=kOutput, calls=%fused_computation.15 | convolution fusion | flops 12017664 | bytes 5181696 | tf_op jit(solution)/shard_map/sgqt,stgd->sgqd/dot_general | solution.py:117
  77.0 1.5 fusion.35
  78.6 0.9 fusion.60
  79.9 24.3 %all-gather.1 = f32[16384,4]{0,1:T(4,128)S(1)} all-gather(f32[512,4]{0,1:T(4,128)S(1)} %fusion.36), channel_id=3, replica_groups=mesh['pool'=32,'exp'=4] {'pool'}, dimensions={0}, use_global_device_ids=true | all-gather | bytes 270336 | tf_op jit(solution)/shard_map/all_gather | solution.py:14
  104.3 22.6 %all-gather = f32[16384,4]{0,1:T(4,128)S(1)} all-gather(f32[512,4]{0,1:T(4,128)S(1)} %select_reduce_fusion.2), channel_id=2, replica_groups=mesh['pool'=32,'exp'=4] {'pool'}, dimensions={0}, use_global_device_ids=true | all-gather | bytes 270336 | tf_op jit(solution)/shard_map/all_gather | solution.py:14
  128.3 23.1 %all-gather.5.cloned.1.call-done = f32[16384,256]{1,0:T(8,128)} async-done(((f32[512,256]{1,0:T(8,128)}), f32[16384,256]{1,0:T(8,128)}) %all-gather.5.cloned.1.call-update) | async-done | bytes 16777232 | tf_op jit(solution)/shard_map/all_gather | solution.py:14
  151.4 1.1 slice.32
  152.7 11.1 %slice.35 = f32[15872,256]{1,0:T(8,128)} slice(f32[16384,256]{1,0:T(8,128)} %all-gather.5.cloned.1.call-done), slice={[512:16384], [0:256]} | slice | bytes 32505856 | tf_op jit(solution)/shard_map/slice | solution.py:16
  163.9 70.2 %while.14 = (s32[]{:T(128)}, f32[512,4]{0,1:T(4,128)S(1)}, f32[512,4]{0,1:T(4,128)S(1)}, f32[512,256]{0,1:T(8,128)S(1)}, f32[31,512,4]{1,2,0:T(4,128)}, /*index=...) while((s32[]{:T(128)}, f32[512,4]{0,1:T(4,128)S(1)}, f32[512,4]{0,1:T(4,128)S(1)}, ...), condition=%wide.region_8.9_spmd, body=%wide.region_7.8_spmd.sunk | while | flops 405506 | bytes 3752029 | solution.py:17
  163.9 0.8 fusion.82
  164.7 1.1 constant_dynamic-slice_fusion.4
  166.9 1.1 constant_dynamic-slice_fusion.4
  168.5 0.7 fusion.82
  169.2 1.1 constant_dynamic-slice_fusion.4
  170.7 0.7 fusion.82
  171.5 1.1 constant_dynamic-slice_fusion.4
  173.7 1.1 constant_dynamic-slice_fusion.4
  176.0 1.1 constant_dynamic-slice_fusion.4
  178.2 1.1 constant_dynamic-slice_fusion.4
  180.5 1.1 constant_dynamic-slice_fusion.4
  182.8 1.1 constant_dynamic-slice_fusion.4
  185.0 1.1 constant_dynamic-slice_fusion.4
  187.3 1.1 constant_dynamic-slice_fusion.4
  189.6 1.1 constant_dynamic-slice_fusion.4
  191.8 1.1 constant_dynamic-slice_fusion.4
  194.1 1.1 constant_dynamic-slice_fusion.4
  196.4 1.1 constant_dynamic-slice_fusion.4
  198.6 1.1 constant_dynamic-slice_fusion.4
  200.9 1.1 constant_dynamic-slice_fusion.4
  203.1 1.1 constant_dynamic-slice_fusion.4
  205.4 1.1 constant_dynamic-slice_fusion.4
  207.7 1.1 constant_dynamic-slice_fusion.4
  209.9 1.1 constant_dynamic-slice_fusion.4
  212.2 1.1 constant_dynamic-slice_fusion.4
  214.5 1.1 constant_dynamic-slice_fusion.4
  216.7 1.1 constant_dynamic-slice_fusion.4
  219.0 1.1 constant_dynamic-slice_fusion.4
  221.3 1.1 constant_dynamic-slice_fusion.4
  223.5 1.1 constant_dynamic-slice_fusion.4
  225.8 1.1 constant_dynamic-slice_fusion.4
  228.0 1.1 constant_dynamic-slice_fusion.4
  230.3 1.1 constant_dynamic-slice_fusion.4
  232.6 1.1 constant_dynamic-slice_fusion.4
  234.3 0.8 fusion.68
  235.3 37.8 %all-reduce.2.cloned.1.call-done = f32[16,1024]{1,0:T(8,128)} async-done(((f32[16,1024]{1,0:T(8,128)}), f32[16,1024]{1,0:T(8,128)}) %all-reduce.2.cloned.1.call-update) | async-done | bytes 65552 | tf_op jit(solution)/shard_map/psum | solution.py:139
  273.1 1.0 multiply_reduce_fusion
  274.1 1.1 fusion.11
  275.2 9.7 %all-to-all-start = ((bf16[32,8,1024]{2,1,0:T(8,128)(2,1)}), bf16[32,8,1024]{2,1,0:T(8,128)(2,1)S(1)}, u32[]{:S(2)}, u32[]{:S(2)}) async-start(bf16[32,8,1024]{2,1,0:T(8,128)(2,1)} %fusion.11), calls=%async_computation | async-start | bytes 1048576 | tf_op jit(solution)/shard_map/all_to_all | solution.py:158
  285.0 11.5 %all-to-all-done = bf16[32,8,1024]{2,1,0:T(8,128)(2,1)S(1)} async-done(((bf16[32,8,1024]{2,1,0:T(8,128)(2,1)}), bf16[32,8,1024]{2,1,0:T(8,128)(2,1)S(1)}, u32[]{:S(2)}, u32[]{:S(2)}) %all-to-all-start) | async-done | bytes 524320 | tf_op jit(solution)/shard_map/all_to_all | solution.py:158
  296.5 1.7 fusion.20
  298.2 2.0 fusion.12
  300.9 3.6 %all-to-all-start.1 = ((bf16[32,8,256]{2,1,0:T(8,128)(2,1)}), bf16[32,8,256]{2,1,0:T(8,128)(2,1)S(1)}, u32[]{:S(2)}, u32[]{:S(2)}) async-start(bf16[32,8,256]{2,1,0:T(8,128)(2,1)} %constant_dynamic-slice_fusion.2), calls=%async_computation.1 | async-start | bytes 262144 | tf_op jit(solution)/shard_map/all_to_all | solution.py:168
  304.8 7.4 %all-to-all-done.1 = bf16[32,8,256]{2,1,0:T(8,128)(2,1)S(1)} async-done(((bf16[32,8,256]{2,1,0:T(8,128)(2,1)}), bf16[32,8,256]{2,1,0:T(8,128)(2,1)S(1)}, u32[]{:S(2)}, u32[]{:S(2)}) %all-to-all-start.1) | async-done | bytes 131104 | tf_op jit(solution)/shard_map/all_to_all | solution.py:168
  312.2 0.8 fusion.17
  (153 shorter events, 41.9 us)
Async XLA Ops:
  6.5 291.6 %copy-start = (bf16[1,512,1024]{2,1,0:T(8,128)(2,1)S(1)}, bf16[1,512,1024]{2,1,0:T(8,128)(2,1)}, u32[]{:S(2)}) copy-start(bf16[1,512,1024]{2,1,0:T(8,128)(2,1)} %param.35) | copy-start | bytes 3145732
  6.5 144.9 %all-gather.5.cloned.1.call-start = ((), (), s32[]{:S(2)}) async-start(), calls=%async_computation.3 | async-start | bytes 17301504 | tf_op jit(solution)/shard_map/all_gather | solution.py:14
  56.1 4.9 %copy-start.6 = (bf16[1024,128]{1,0:T(8,128)(2,1)S(1)}, bf16[1024,128]{1,0:T(8,128)(2,1)}, u32[]{:S(2)}) copy-start(bf16[1024,128]{1,0:T(8,128)(2,1)} %param.28) | copy-start | bytes 786436
  76.7 50.9 %copy-start.3 = (s32[16,8]{0,1:T(8,128)S(1)}, s32[16,8]{0,1:T(8,128)}, u32[]{:S(2)}) copy-start(s32[16,8]{0,1:T(8,128)} %param.31) | copy-start | bytes 1540
  76.7 51.6 %copy-start.5 = (bf16[1024]{0:T(1024)(128)(2,1)S(1)}, bf16[1024]{0:T(1024)(128)(2,1)}, u32[]{:S(2)}) copy-start(bf16[1024]{0:T(1024)(128)(2,1)} %param.30) | copy-start | bytes 6148
  78.5 194.6 %all-reduce.2.cloned.1.call-start = ((), (), s32[]{:S(2)}) async-start(), calls=%async_computation.2 | async-start | bytes 131072 | tf_op jit(solution)/shard_map/psum | solution.py:139
  163.9 70.4 %copy-start.1 = (bf16[256,1024]{1,0:T(8,128)(2,1)S(1)}, bf16[256,1024]{1,0:T(8,128)(2,1)}, u32[]{:S(2)}) copy-start(bf16[256,1024]{1,0:T(8,128)(2,1)} %param.29) | copy-start | bytes 1572868
  163.9 109.2 %copy-start.2 = (bf16[16,1024]{1,0:T(8,128)(2,1)S(1)}, bf16[16,1024]{1,0:T(8,128)(2,1)}, u32[]{:S(2)}) copy-start(bf16[16,1024]{1,0:T(8,128)(2,1)} %param.19) | copy-start | bytes 98308
  163.9 121.0 %copy-start.4 = (f32[16,8]{0,1:T(8,128)S(1)}, f32[16,8]{0,1:T(8,128)}, u32[]{:S(2)}) copy-start(f32[16,8]{0,1:T(8,128)} %param.32) | copy-start | bytes 1540
  275.2 21.3 %all-to-all-start = ((bf16[32,8,1024]{2,1,0:T(8,128)(2,1)}), bf16[32,8,1024]{2,1,0:T(8,128)(2,1)S(1)}, u32[]{:S(2)}, u32[]{:S(2)}) async-start(bf16[32,8,1024]{2,1,0:T(8,128)(2,1)} %fusion.11), calls=%async_computation | async-start | bytes 1048576 | tf_op jit(solution)/shard_map/all_to_all | solution.py:158
  300.9 11.3 %all-to-all-start.1 = ((bf16[32,8,256]{2,1,0:T(8,128)(2,1)}), bf16[32,8,256]{2,1,0:T(8,128)(2,1)S(1)}, u32[]{:S(2)}, u32[]{:S(2)}) async-start(bf16[32,8,256]{2,1,0:T(8,128)(2,1)} %constant_dynamic-slice_fusion.2), calls=%async_computation.1 | async-start | bytes 262144 | tf_op jit(solution)/shard_map/all_to_all | solution.py:168
Sparse Core Ops, SparseCore 0:
  78.6 72.7 all-gather.4
  235.3 37.7 all-reduce.1
where the time goes:
time: 324 us; the launch traced here: 320 us
  waiting for transfers between devices  79.9 us (25%)
  blocking collectives  74.6 us (23%)
  local copies, waits for them, and re-layouts  70 us (22%)
  other arithmetic  42 us (13%)
  matrix products  25.4 us (8%)
  between operations  13.7 us (4%)
  starting transfers between devices  13.4 us (4%)
    all_gather x2, blocking collectives, merged(): pieces = jax.tree.map(lambda part: lax.all_gather(part, axis), value)  47 us
    dynamic_slice x62, local copies, waits for them, and re-layouts, merged(): lax.scan(lambda so_far, piece: (join(so_far, piece), None), head, tail)  39.6 us
    psum x1, waiting for transfers between devices, on_device(): lax.psum(jnp.dot(attended, w_out, preferred_element_type=jnp.float32), 'e...  37.8 us
    all_gather x1, blocking collectives, on_device(): all_queries = lax.all_gather(queries, 'pool', axis=0, tiled=True)  27.6 us
    all_gather x1, waiting for transfers between devices, merged(): pieces = jax.tree.map(lambda part: lax.all_gather(part, axis), value)  23.1 us
    add x31, other arithmetic, merge_pair(): return (row_top, sum_a * weight_a + sum_b * weight_b, merged_out)  22.5 us
    unnamed x18, local copies, waits for them, and re-layouts  13 us
    slice x3, local copies, waits for them, and re-layouts, merged(): tail = jax.tree.map(lambda part: part[1:], pieces)  11.9 us
  transfers between devices with their start and end apart: 4, of which 4 were waited for; matrix products, arithmetic and copies ran while one was open for 1% of the time, Pallas kernels for 0%

commit v1 on v0

--- a/solution.py
+++ b/solution.py
@@ -8,6 +8,11 @@
 EPSILON = 1e-05
 SCORE_SCALE = 0.125
 HIGHEST = lax.Precision.HIGHEST
+
+
+def summed_here(x, mesh_axis):
+    parts = lax.all_gather(x, mesh_axis)
+    return jnp.sum(parts, axis=0)
 
 
 def merged(value, axis, join):
@@ -136,7 +141,7 @@
     total_sum = lax.dynamic_slice_in_dim(all_sum, row_start, req_dev, 0)
     accum = lax.dynamic_slice_in_dim(all_out, row_start, req_dev, 0)
     attended = (accum / jnp.repeat(total_sum, HEAD_SIZE, axis=-1)).astype(jnp.bfloat16)
-    projected = lax.psum(jnp.dot(attended, w_out, preferred_element_type=jnp.float32), "exp")
+    projected = summed_here(jnp.dot(attended, w_out, preferred_element_type=jnp.float32), "exp")
     mixed = x_rows + projected
     normed_moe = rms_scale(mixed, norm_moe.astype(jnp.float32)).astype(jnp.bfloat16)
     top_count = expert_ids.shape[1]

time: 324 us -> 292 us (0.901)
  waiting for transfers between devices: 79.9 us -> 42 us
  blocking collectives: 74.6 us -> 84.9 us
    psum x1 -> x0, waiting for transfers between devices: 37.8 us -> none  [on_device(): lax.psum(jnp.dot(attended, w_out, preferred_element_type=jnp.float32), 'e...]
    all_gather x0 -> x1, blocking collectives: none -> 10.3 us  [summed_here(): parts = lax.all_gather(x, mesh_axis)]
  transfers between devices with their start and end apart: 4 -> 3, of which waited for: 4 -> 3; matrix products, arithmetic and copies ran while one was open for 1% -> 1% of each run, Pallas kernels for 0% -> 0%
where the time goes in v1:
time: 292 us; the launch traced here: 289 us
  blocking collectives  84.9 us (29%)
  local copies, waits for them, and re-layouts  70 us (24%)
  waiting for transfers between devices  42 us (14%)
  other arithmetic  41.2 us (14%)
  matrix products  24.7 us (8%)
  between operations  13.7 us (5%)
  starting transfers between devices  11.3 us (4%)
    all_gather x2, blocking collectives, merged(): pieces = jax.tree.map(lambda part: lax.all_gather(part, axis), value)  47 us
    dynamic_slice x62, local copies, waits for them, and re-layouts, merged(): lax.scan(lambda so_far, piece: (join(so_far, piece), None), head, tail)  39.6 us
    all_gather x1, blocking collectives, on_device(): all_queries = lax.all_gather(queries, 'pool', axis=0, tiled=True)  27.6 us
    all_gather x1, waiting for transfers between devices, merged(): pieces = jax.tree.map(lambda part: lax.all_gather(part, axis), value)  23 us
    add x31, other arithmetic, merge_pair(): return (row_top, sum_a * weight_a + sum_b * weight_b, merged_out)  22.5 us
    unnamed x18, local copies, waits for them, and re-layouts  13 us
    slice x3, local copies, waits for them, and re-layouts, merged(): tail = jax.tree.map(lambda part: part[1:], pieces)  11.9 us
    all_to_all x1, waiting for transfers between devices, on_device(): lax.all_to_all(outgoing, 'pool', split_axis=0, concat_axis=0, tiled=True)  11.5 us
  transfers between devices with their start and end apart: 3, of which 3 were waited for; matrix products, arithmetic and copies ran while one was open for 1% of the time, Pallas kernels for 0%

profile of v1, /device:TPU:1, one launch (start us, length us, event | category | flops | bytes accessed | tf_op | source)
XLA Modules:
  0.0 288.7 jit_solution(3799352625239531753)
XLA Ops:
  6.5 6.6 %select_reduce_fusion = s32[144]{0:T(256)S(1)} fusion(s32[65536]{0:T(1024)} %bitcast.89, s32[144]{0:T(256)S(1)} %iota_add_fusion), kind=kLoop, calls=%fused_computation.10 | loop fusion | flops 28311408 | bytes 263296 | tf_op jit(solution)/shard_map/reduce_sum | solution.py:98
  13.3 0.9 select_reduce_fusion.3
  14.9 0.9 fusion.46
  15.8 1.3 convolution_convert_fusion.5
  17.1 27.6 %all_gather.27 = bf16[512,256]{1,0:T(8,128)(2,1)S(1)} all-gather(bf16[16,256]{1,0:T(8,128)(2,1)S(1)} %convolution_convert_fusion.5), channel_id=1, replica_groups=mesh['pool'=32,'exp'=4] {'pool'}, dimensions={0}, use_global_device_ids=true | all-gather | bytes 270336 | tf_op jit(solution)/shard_map/all_gather | solution.py:73
  45.1 3.5 %convolution_convert_fusion.1 = bf16[2048,128]{1,0:T(8,128)(2,1)S(1)} fusion(bf16[2048,1024]{1,0:T(8,128)(2,1)} %bitcast.91, bf16[1024,128]{1,0:T(8,128)(2,1)} %param.27), kind=kOutput, calls=%fused_computation.20 | convolution fusion | flops 537133056 | bytes 4980736 | tf_op jit(solution)/shard_map/dot_general | solution.py:77
  49.6 6.4 %copy.75 = bf16[128,128,128]{1,2,0:T(8,128)(2,1)} copy(bf16[128,128,128]{2,1,0:T(8,128)(2,1)} %param.22) | data formatting | bytes 8388608 | tf_op args[3]
  56.1 3.7 %fusion.67 = (f32[144,2,2]{2,1,0:T(2,128)S(1)}, f32[144,2,2,128]{3,2,1,0:T(2,128)S(1)}) fusion(bf16[144,2,2,64]{3,2,1,0:T(2,128)(2,1)S(1)} %reshape.185, bf16[16,128,2,64]{1,3,2,0:T(8,128)(2,1)S(1)} %copy.77, bf16[128,128,2,64]{1,3,2,0:T(8,128)(2,1)} %bitcast.85, pred[144,128]{1,0:T(8,128)(4,1)S(1)} %add_compare_fusion), kind=kOutput, calls=%fused_computation.105 | convolution fusion | flops 12017088 | bytes 5107968 | tf_op jit(solution)/shard_map/sgqd,stgd->sgqt/dot_general | solution.py:113
  61.0 3.4 %convolution_convert_fusion = bf16[2048,128]{1,0:T(8,128)(2,1)S(1)} fusion(bf16[2048,1024]{1,0:T(8,128)(2,1)} %bitcast.92, bf16[1024,128]{1,0:T(8,128)(2,1)S(1)} %copy-done.6), kind=kOutput, calls=%fused_computation.19 | convolution fusion | flops 537133056 | bytes 4980736 | tf_op jit(solution)/shard_map/dot_general | solution.py:82
  65.5 6.4 %copy.80 = bf16[128,128,128]{1,2,0:T(8,128)(2,1)} copy(bf16[128,128,128]{2,1,0:T(8,128)(2,1)} %param.23) | data formatting | bytes 8388608 | tf_op args[4]
  71.9 4.8 %fusion.7 = f32[144,2,2,64]{3,2,1,0:T(2,128)S(1)} fusion(bf16[16,128,2,64]{1,3,2,0:T(8,128)(2,1)S(1)} %copy.82, bf16[128,128,2,64]{1,3,2,0:T(8,128)(2,1)} %bitcast.86, f32[144,2,2,128]{3,2,1,0:T(2,128)S(1)} %get-tuple-element.103, pred[144,128]{1,0:T(8,128)(4,1)S(1)} %add_compare_fusion, f32[144,2,2]{2,1,0:T(2,128)S(1)} %get-tuple-element.102), kind=kOutput, calls=%fused_computation.15 | convolution fusion | flops 12017664 | bytes 5181696 | tf_op jit(solution)/shard_map/sgqt,stgd->sgqd/dot_general | solution.py:122
  77.0 1.5 fusion.35
  78.5 0.9 fusion.60
  79.8 24.3 %all-gather.1 = f32[16384,4]{0,1:T(4,128)S(1)} all-gather(f32[512,4]{0,1:T(4,128)S(1)} %fusion.36), channel_id=3, replica_groups=mesh['pool'=32,'exp'=4] {'pool'}, dimensions={0}, use_global_device_ids=true | all-gather | bytes 270336 | tf_op jit(solution)/shard_map/all_gather | solution.py:19
  104.2 22.6 %all-gather = f32[16384,4]{0,1:T(4,128)S(1)} all-gather(f32[512,4]{0,1:T(4,128)S(1)} %select_reduce_fusion.2), channel_id=2, replica_groups=mesh['pool'=32,'exp'=4] {'pool'}, dimensions={0}, use_global_device_ids=true | all-gather | bytes 270336 | tf_op jit(solution)/shard_map/all_gather | solution.py:19
  128.4 23.0 %all-gather.6.cloned.1.call-done = f32[16384,256]{1,0:T(8,128)} async-done(((f32[512,256]{1,0:T(8,128)}), f32[16384,256]{1,0:T(8,128)}) %all-gather.6.cloned.1.call-update) | async-done | bytes 16777232 | tf_op jit(solution)/shard_map/all_gather | solution.py:19
  151.4 1.1 slice.32
  152.7 11.1 %slice.35 = f32[15872,256]{1,0:T(8,128)} slice(f32[16384,256]{1,0:T(8,128)} %all-gather.6.cloned.1.call-done), slice={[512:16384], [0:256]} | slice | bytes 32505856 | tf_op jit(solution)/shard_map/slice | solution.py:21
  163.8 70.2 %while.14 = (s32[]{:T(128)}, f32[512,4]{0,1:T(4,128)S(1)}, f32[512,4]{0,1:T(4,128)S(1)}, f32[512,256]{0,1:T(8,128)S(1)}, f32[31,512,4]{1,2,0:T(4,128)}, /*index=...) while((s32[]{:T(128)}, f32[512,4]{0,1:T(4,128)S(1)}, f32[512,4]{0,1:T(4,128)S(1)}, ...), condition=%wide.region_8.9_spmd, body=%wide.region_7.8_spmd.sunk | while | flops 405506 | bytes 3752029 | solution.py:22
  163.8 0.8 fusion.82
  164.6 1.1 constant_dynamic-slice_fusion.4
  166.2 0.7 fusion.82
  166.9 1.1 constant_dynamic-slice_fusion.4
  168.4 0.7 fusion.82
  169.2 1.1 constant_dynamic-slice_fusion.4
  170.7 0.7 fusion.82
  171.4 1.1 constant_dynamic-slice_fusion.4
  173.0 0.7 fusion.82
  173.7 1.1 constant_dynamic-slice_fusion.4
  175.9 1.1 constant_dynamic-slice_fusion.4
  178.2 1.1 constant_dynamic-slice_fusion.4
  180.5 1.1 constant_dynamic-slice_fusion.4
  182.7 1.1 constant_dynamic-slice_fusion.4
  185.0 1.1 constant_dynamic-slice_fusion.4
  187.3 1.1 constant_dynamic-slice_fusion.4
  189.5 1.1 constant_dynamic-slice_fusion.4
  191.8 1.1 constant_dynamic-slice_fusion.4
  194.1 1.1 constant_dynamic-slice_fusion.4
  196.3 1.1 constant_dynamic-slice_fusion.4
  198.6 1.1 constant_dynamic-slice_fusion.4
  200.8 1.1 constant_dynamic-slice_fusion.4
  203.1 1.1 constant_dynamic-slice_fusion.4
  205.4 1.1 constant_dynamic-slice_fusion.4
  207.6 1.1 constant_dynamic-slice_fusion.4
  209.9 1.1 constant_dynamic-slice_fusion.4
  212.2 1.1 constant_dynamic-slice_fusion.4
  214.4 1.1 constant_dynamic-slice_fusion.4
  216.7 1.1 constant_dynamic-slice_fusion.4
  219.0 1.1 constant_dynamic-slice_fusion.4
  221.2 1.1 constant_dynamic-slice_fusion.4
  223.5 1.1 constant_dynamic-slice_fusion.4
  225.7 1.1 constant_dynamic-slice_fusion.4
  228.0 1.1 constant_dynamic-slice_fusion.4
  230.3 1.1 constant_dynamic-slice_fusion.4
  232.5 1.1 constant_dynamic-slice_fusion.4
  234.5 10.3 %all-gather.3 = f32[64,1024]{1,0:T(8,128)S(1)} all-gather(f32[16,1024]{1,0:T(8,128)S(1)} %fusion.68), channel_id=5, replica_groups=mesh['pool'=32,'exp'=4] {'exp'}, dimensions={0}, use_global_device_ids=true | all-gather | bytes 327680 | tf_op jit(solution)/shard_map/all_gather | solution.py:14
  245.0 1.1 fusion.11
  246.1 7.6 %all-to-all-start = ((bf16[32,8,1024]{2,1,0:T(8,128)(2,1)}), bf16[32,8,1024]{2,1,0:T(8,128)(2,1)S(1)}, u32[]{:S(2)}, u32[]{:S(2)}) async-start(bf16[32,8,1024]{2,1,0:T(8,128)(2,1)} %fusion.11), calls=%async_computation | async-start | bytes 1048576 | tf_op jit(solution)/shard_map/all_to_all | solution.py:163
  253.8 11.5 %all-to-all-done = bf16[32,8,1024]{2,1,0:T(8,128)(2,1)S(1)} async-done(((bf16[32,8,1024]{2,1,0:T(8,128)(2,1)}), bf16[32,8,1024]{2,1,0:T(8,128)(2,1)S(1)}, u32[]{:S(2)}, u32[]{:S(2)}) %all-to-all-start) | async-done | bytes 524320 | tf_op jit(solution)/shard_map/all_to_all | solution.py:163
  265.4 1.7 fusion.20
  267.0 2.0 fusion.12
  269.7 3.6 %all-to-all-start.1 = ((bf16[32,8,256]{2,1,0:T(8,128)(2,1)}), bf16[32,8,256]{2,1,0:T(8,128)(2,1)S(1)}, u32[]{:S(2)}, u32[]{:S(2)}) async-start(bf16[32,8,256]{2,1,0:T(8,128)(2,1)} %constant_dynamic-slice_fusion.2), calls=%async_computation.1 | async-start | bytes 262144 | tf_op jit(solution)/shard_map/all_to_all | solution.py:173
  273.7 7.4 %all-to-all-done.1 = bf16[32,8,256]{2,1,0:T(8,128)(2,1)S(1)} async-done(((bf16[32,8,256]{2,1,0:T(8,128)(2,1)}), bf16[32,8,256]{2,1,0:T(8,128)(2,1)S(1)}, u32[]{:S(2)}, u32[]{:S(2)}) %all-to-all-start.1) | async-done | bytes 131104 | tf_op jit(solution)/shard_map/all_to_all | solution.py:173
  281.1 0.8 fusion.17
  (152 shorter events, 40.7 us)
Async XLA Ops:
  6.5 260.5 %copy-start = (bf16[1,512,1024]{2,1,0:T(8,128)(2,1)S(1)}, bf16[1,512,1024]{2,1,0:T(8,128)(2,1)}, u32[]{:S(2)}) copy-start(bf16[1,512,1024]{2,1,0:T(8,128)(2,1)} %param.35) | copy-start | bytes 3145732
  6.5 144.9 %all-gather.6.cloned.1.call-start = ((), (), s32[]{:S(2)}) async-start(), calls=%async_computation.2 | async-start | bytes 17301504 | tf_op jit(solution)/shard_map/all_gather | solution.py:19
  56.1 4.9 %copy-start.6 = (bf16[1024,128]{1,0:T(8,128)(2,1)S(1)}, bf16[1024,128]{1,0:T(8,128)(2,1)}, u32[]{:S(2)}) copy-start(bf16[1024,128]{1,0:T(8,128)(2,1)} %param.28) | copy-start | bytes 786436
  76.7 50.8 %copy-start.3 = (s32[16,8]{0,1:T(8,128)S(1)}, s32[16,8]{0,1:T(8,128)}, u32[]{:S(2)}) copy-start(s32[16,8]{0,1:T(8,128)} %param.31) | copy-start | bytes 1540
  76.7 51.5 %copy-start.5 = (bf16[1024]{0:T(1024)(128)(2,1)S(1)}, bf16[1024]{0:T(1024)(128)(2,1)}, u32[]{:S(2)}) copy-start(bf16[1024]{0:T(1024)(128)(2,1)} %param.30) | copy-start | bytes 6148
  163.8 70.4 %copy-start.1 = (bf16[256,1024]{1,0:T(8,128)(2,1)S(1)}, bf16[256,1024]{1,0:T(8,128)(2,1)}, u32[]{:S(2)}) copy-start(bf16[256,1024]{1,0:T(8,128)(2,1)} %param.29) | copy-start | bytes 1572868
  163.8 81.0 %copy-start.2 = (bf16[16,1024]{1,0:T(8,128)(2,1)S(1)}, bf16[16,1024]{1,0:T(8,128)(2,1)}, u32[]{:S(2)}) copy-start(bf16[16,1024]{1,0:T(8,128)(2,1)} %param.19) | copy-start | bytes 98308
  163.8 89.9 %copy-start.4 = (f32[16,8]{0,1:T(8,128)S(1)}, f32[16,8]{0,1:T(8,128)}, u32[]{:S(2)}) copy-start(f32[16,8]{0,1:T(8,128)} %param.32) | copy-start | bytes 1540
  246.1 19.3 %all-to-all-start = ((bf16[32,8,1024]{2,1,0:T(8,128)(2,1)}), bf16[32,8,1024]{2,1,0:T(8,128)(2,1)S(1)}, u32[]{:S(2)}, u32[]{:S(2)}) async-start(bf16[32,8,1024]{2,1,0:T(8,128)(2,1)} %fusion.11), calls=%async_computation | async-start | bytes 1048576 | tf_op jit(solution)/shard_map/all_to_all | solution.py:163
  269.7 11.3 %all-to-all-start.1 = ((bf16[32,8,256]{2,1,0:T(8,128)(2,1)}), bf16[32,8,256]{2,1,0:T(8,128)(2,1)S(1)}, u32[]{:S(2)}, u32[]{:S(2)}) async-start(bf16[32,8,256]{2,1,0:T(8,128)(2,1)} %constant_dynamic-slice_fusion.2), calls=%async_computation.1 | async-start | bytes 262144 | tf_op jit(solution)/shard_map/all_to_all | solution.py:173
Sparse Core Ops, SparseCore 0:
  78.6 72.7 all-gather.5
